TPU v7x, 128 devices: a whole 4x4x4 slice. The times are simulated.
128 devices in a mesh: seq: 16 (over z_lo, x, core), res: 8 (over y, z_hi).
Axes of the slice: x: 4, y: 4, z: 4 (z_hi: 2, z_lo: 2; z = z_hi * 2 + z_lo), core: 2. Of those that a mesh axis runs over, the one named last changes fastest.
Arguments:
- states: bfloat16 [512, 256, 768], P('seq', 'res'), may hold values from -6 to 6
- row_query: bfloat16 [768, 768], replicated, as said below
- row_key: bfloat16 [768, 768], replicated
- row_value: bfloat16 [768, 768], replicated, may hold values from -0.21875 to 0.21875
- row_out: bfloat16 [768, 768], replicated, may hold values from -0.21875 to 0.21875
- col_query: bfloat16 [768, 768], replicated, as said below
- col_key: bfloat16 [768, 768], replicated
- col_value: bfloat16 [768, 768], replicated, may hold values from -0.21875 to 0.21875
- col_out: bfloat16 [768, 768], replicated, may hold values from -0.21875 to 0.21875
Outputs:
- updated: bfloat16 [512, 256, 768], P('seq', 'res')
Inputs may be any that keep to these rules, and one draw needn't show every extreme that they name: No bound on the size of row_query and row_key entries or of the scores they give is promised. No bound on the size of col_query and col_key entries or of the scores they give is promised.
All inputs are finite; a program needn't handle non-finite values.
Results may differ from a plain program's by a relative error of at most 0.02.
Values may be sent and summed in bfloat16 or wider, within the bound.
A program may use at most 128 MiB of HBM per device.

v0:
```python
import math
import jax
import jax.numpy as jnp
from jax import lax
from jax.sharding import PartitionSpec as P

D = 768
HEADS = 12


def normalize(states):
    values = states.astype(jnp.float32)
    center = values - jnp.mean(values, axis=-1, keepdims=True)
    spread = jnp.mean(center * center, axis=-1, keepdims=True)
    return (center * lax.rsqrt(spread + 1e-05)).astype(jnp.bfloat16)


def project(inputs, weight):
    return jnp.dot(inputs, weight, preferred_element_type=jnp.float32)


def split_heads(field):
    return field.reshape(field.shape[0], field.shape[1], HEADS, D // HEADS)


def on_device(
    states, row_query, row_key, row_value, row_out, col_query, col_key, col_value, col_out
):
    row_count, col_count = (states.shape[0], states.shape[1])
    head_dim = D // HEADS
    all_rows = row_count * lax.axis_size("seq")
    tied_scale = head_dim ** (-0.5) / math.sqrt(all_rows)
    normed = normalize(states)
    q1 = project(normed, row_query).astype(jnp.bfloat16)
    k1 = project(normed, row_key).astype(jnp.bfloat16)
    v1 = project(normed, row_value).astype(jnp.bfloat16)
    q_moved, k_moved, v_moved = (
        lax.all_to_all(q1, "res", split_axis=0, concat_axis=1, tiled=True),
        lax.all_to_all(k1, "res", split_axis=0, concat_axis=1, tiled=True),
        lax.all_to_all(v1, "res", split_axis=0, concat_axis=1, tiled=True),
    )
    partial_value = (
        jnp.einsum(
            "rihd,rjhd->hij",
            split_heads(q_moved),
            split_heads(k_moved),
            preferred_element_type=jnp.float32,
        )
        * tied_scale
    )
    tied = lax.psum(partial_value, ("seq", "res"))
    prob1 = jax.nn.softmax(tied, axis=-1).astype(jnp.bfloat16)
    o_moved = jnp.einsum(
        "hij,rjhd->rihd", prob1, split_heads(v_moved), preferred_element_type=jnp.float32
    ).astype(jnp.bfloat16)
    o_moved = o_moved.reshape(o_moved.shape[0], o_moved.shape[1], D)
    o1 = lax.all_to_all(o_moved, "res", split_axis=1, concat_axis=0, tiled=True)
    mid = (states.astype(jnp.float32) + project(o1, row_out)).astype(jnp.bfloat16)
    normed2 = normalize(mid)
    q2 = project(normed2, col_query).astype(jnp.bfloat16)
    k2 = project(normed2, col_key).astype(jnp.bfloat16)
    v2 = project(normed2, col_value).astype(jnp.bfloat16)
    q_cols, k_cols, v_cols = (
        lax.all_to_all(q2, "seq", split_axis=1, concat_axis=0, tiled=True),
        lax.all_to_all(k2, "seq", split_axis=1, concat_axis=0, tiled=True),
        lax.all_to_all(v2, "seq", split_axis=1, concat_axis=0, tiled=True),
    )
    gathered_rows, local_cols = (q_cols.shape[0], q_cols.shape[1])

    def arrange(field):
        return field.reshape(gathered_rows, local_cols, HEADS, head_dim).transpose(1, 0, 2, 3)

    def attend(triple):
        query_col, key_col, value_col = triple
        score = jnp.einsum(
            "rhd,shd->hrs", query_col, key_col, preferred_element_type=jnp.float32
        ) * head_dim ** (-0.5)
        prob2 = jax.nn.softmax(score, axis=-1).astype(jnp.bfloat16)
        return jnp.einsum(
            "hrs,shd->rhd", prob2, value_col, preferred_element_type=jnp.float32
        ).astype(jnp.bfloat16)

    o2 = lax.map(attend, (arrange(q_cols), arrange(k_cols), arrange(v_cols)))
    o2 = o2.reshape(local_cols, gathered_rows, D).transpose(1, 0, 2)
    colupd = project(o2, col_out).astype(jnp.bfloat16)
    colupd = lax.all_to_all(colupd, "seq", split_axis=0, concat_axis=1, tiled=True)
    return (mid.astype(jnp.float32) + colupd.astype(jnp.float32)).astype(jnp.bfloat16)


def solution(mesh):
    placed = (P("seq", "res", None), P(), P(), P(), P(), P(), P(), P(), P())
    return jax.shard_map(
        on_device, mesh=mesh, in_specs=placed, out_specs=P("seq", "res", None), check_vma=False
    )
```

profile of v0, /device:TPU:1, one launch (start us, length us, event | category | flops | bytes accessed | tf_op | source)
XLA Modules:
  0.0 487.7 jit_solution(7350773890253013936)
XLA Ops:
  11.7 8.3 %all-to-all-start.1 = ((bf16[32,32,768]{2,1,0:T(8,128)(2,1)}), bf16[32,32,768]{2,1,0:T(8,128)(2,1)}, u32[]{:S(2)}, u32[]{:S(2)}) async-start(bf16[32,32,768]{2,1,0:T(8,128)(2,1)} %convolution_convert_fusion.5), calls=%async_computation.1 | async-start | bytes 3145728 | tf_op jit(solution)/shard_map/all_to_all | solution.py:38
  20.1 3.9 convolution_convert_fusion.4
  23.9 19.3 %all-to-all-done.1 = bf16[32,32,768]{2,1,0:T(8,128)(2,1)} async-done(((bf16[32,32,768]{2,1,0:T(8,128)(2,1)}), bf16[32,32,768]{2,1,0:T(8,128)(2,1)}, u32[]{:S(2)}, u32[]{:S(2)}) %all-to-all-start.1) | async-done | bytes 1572896 | tf_op jit(solution)/shard_map/all_to_all | solution.py:38
  43.2 4.3 all-to-all-start.2
  50.3 5.9 %reshape.63 = bf16[4,256,12,64]{3,2,1,0:T(8,128)(2,1)} reshape(bf16[4,8,32,768]{3,2,1,0:T(8,128)(2,1)} %bitcast.147) | data formatting | bytes 3145728 | tf_op jit(solution)/shard_map/reshape | solution.py:23
  56.2 13.5 %all-to-all-done.2 = bf16[32,32,768]{2,1,0:T(8,128)(2,1)} async-done(((bf16[32,32,768]{2,1,0:T(8,128)(2,1)}), bf16[32,32,768]{2,1,0:T(8,128)(2,1)}, u32[]{:S(2)}, u32[]{:S(2)}) %all-to-all-start.2) | async-done | bytes 1572896 | tf_op jit(solution)/shard_map/all_to_all | solution.py:39
  72.3 5.9 %reshape.64 = bf16[4,256,12,64]{3,2,1,0:T(8,128)(2,1)} reshape(bf16[4,8,32,768]{3,2,1,0:T(8,128)(2,1)} %bitcast.148) | data formatting | bytes 3145728 | tf_op jit(solution)/shard_map/reshape | solution.py:23
  78.2 6.7 %bitcast_multiply_fusion = f32[12,256,256]{2,1,0:T(8,128)} fusion(bf16[4,256,12,64]{3,2,1,0:T(8,128)(2,1)} %reshape.64, bf16[4,256,12,64]{3,2,1,0:T(8,128)(2,1)} %reshape.63), kind=kOutput, calls=%fused_computation.43 | convolution fusion | flops 403439616 | bytes 6291456 | tf_op jit(solution)/shard_map/rihd,rjhd->hij/dot_general | solution.py:43
  87.7 26.8 %all_to_all.117 = bf16[32,32,768]{2,1,0:T(8,128)(2,1)S(1)} all-to-all(bf16[32,32,768]{2,1,0:T(8,128)(2,1)S(1)} %convolution_convert_fusion.6), channel_id=1, replica_groups=mesh['seq'=16,'res'=8] {'res'}, dimensions={0} | all-to-all | bytes 3145728 | tf_op jit(solution)/shard_map/all_to_all | solution.py:40
  115.8 5.9 %reshape.62 = bf16[4,256,12,64]{3,2,1,0:T(8,128)(2,1)} reshape(bf16[4,8,32,768]{3,2,1,0:T(8,128)(2,1)} %bitcast.149) | data formatting | bytes 3145728 | tf_op jit(solution)/shard_map/reshape | solution.py:23
  121.7 123.8 %all-reduce.2.cloned.1.call-done = f32[12,256,256]{2,1,0:T(8,128)} async-done(((f32[12,256,256]{2,1,0:T(8,128)}), f32[12,256,256]{2,1,0:T(8,128)}) %all-reduce.2.cloned.1.call-update) | async-done | bytes 3145744 | tf_op jit(solution)/shard_map/psum | solution.py:51
  245.5 3.8 fusion.92
  249.3 12.5 %fusion.63 = bf16[4,256,12,64]{1,3,0,2:T(8,128)(2,1)} fusion(f32[12,256]{1,0:T(8,128)S(1)} %fusion.92, bf16[4,256,12,64]{3,2,1,0:T(8,128)(2,1)} %reshape.62, f32[12,256,256]{2,1,0:T(8,128)} %all-reduce.2.cloned.1.call-done), kind=kOutput, calls=%fused_computation.68 | convolution fusion | flops 405802240 | bytes 6303744 | tf_op jit(solution)/shard_map/hij,rjhd->rihd/dot_general | solution.py:53
  268.2 25.9 %all_to_all.118 = bf16[4,256,768]{2,0,1:T(4,128)(2,1)S(1)} all-to-all(bf16[4,256,768]{2,0,1:T(4,128)(2,1)} %copy.42), channel_id=1, replica_groups=mesh['seq'=16,'res'=8] {'res'}, dimensions={1} | all-to-all | bytes 3145728 | tf_op jit(solution)/shard_map/all_to_all | solution.py:57
  301.3 6.3 %all-to-all-start.6 = ((bf16[32,32,768]{2,0,1:T(8,128)(2,1)}), bf16[32,32,768]{2,0,1:T(8,128)(2,1)S(1)}, u32[]{:S(2)}, u32[]{:S(2)}) async-start(bf16[32,32,768]{2,0,1:T(8,128)(2,1)} %copy.49), calls=%async_computation.6 | async-start | bytes 3145728 | tf_op jit(solution)/shard_map/all_to_all | solution.py:65
  312.9 16.3 %all-to-all-done.6 = bf16[32,32,768]{2,0,1:T(8,128)(2,1)S(1)} async-done(((bf16[32,32,768]{2,0,1:T(8,128)(2,1)}), bf16[32,32,768]{2,0,1:T(8,128)(2,1)S(1)}, u32[]{:S(2)}, u32[]{:S(2)}) %all-to-all-start.6) | async-done | bytes 1572896 | tf_op jit(solution)/shard_map/all_to_all | solution.py:65
  329.1 4.9 all-to-all-start.5
  339.3 16.4 %all-to-all-done.5 = bf16[32,32,768]{2,0,1:T(8,128)(2,1)} async-done(((bf16[32,32,768]{2,0,1:T(8,128)(2,1)}), bf16[32,32,768]{2,0,1:T(8,128)(2,1)}, u32[]{:S(2)}, u32[]{:S(2)}) %all-to-all-start.5) | async-done | bytes 1572896 | tf_op jit(solution)/shard_map/all_to_all | solution.py:64
  355.7 13.4 %all-to-all-start.4 = ((bf16[32,32,768]{2,0,1:T(8,128)(2,1)}), bf16[32,32,768]{2,0,1:T(8,128)(2,1)}, u32[]{:S(2)}, u32[]{:S(2)}) async-start(bf16[32,32,768]{2,0,1:T(8,128)(2,1)} %copy.45), calls=%async_computation.4 | async-start | bytes 3145728 | tf_op jit(solution)/shard_map/all_to_all | solution.py:66
  370.4 5.9 %reshape.68 = bf16[512,2,12,64]{3,2,0,1:T(8,128)(2,1)} reshape(bf16[16,32,2,768]{3,1,0,2:T(8,128)(2,1)} %bitcast.150) | data formatting | bytes 3145728 | tf_op jit(solution)/shard_map/reshape | solution.py:71
  376.3 5.3 %copy.53 = bf16[2,512,12,64]{1,3,2,0:T(8,128)(2,1)} copy(bf16[2,512,12,64]{3,2,1,0:T(8,128)(2,1)} %bitcast.140) | data formatting | bytes 3145728 | tf_op jit(solution)/shard_map/while | solution.py:83
  383.2 3.9 reshape.67
  387.0 5.3 %copy.52 = bf16[2,512,12,64]{1,3,2,0:T(8,128)(2,1)} copy(bf16[2,512,12,64]{3,2,1,0:T(8,128)(2,1)} %bitcast.141) | data formatting | bytes 3145728 | tf_op jit(solution)/shard_map/while | solution.py:83
  393.9 3.9 reshape.66
  397.8 5.5 %copy.51 = bf16[2,512,12,64]{1,3,2,0:T(8,128)(2,1)} copy(bf16[2,512,12,64]{3,2,1,0:T(8,128)(2,1)} %bitcast.142) | data formatting | bytes 3145728 | tf_op jit(solution)/shard_map/while | solution.py:83
  403.2 32.3 %while.10 = (s32[]{:T(128)}, bf16[2,512,12,64]{1,3,2,0:T(8,128)(2,1)S(1)}, bf16[2,512,12,64]{1,3,2,0:T(8,128)(2,1)}, bf16[2,512,12,64]{1,3,2,0:T(8,128)(2,1)}, bf16[2,512,12,64]{1,3,2,0:T(8,128)(2,1)}, /*index=5*/s32[]{:T(128)}) while((s32[]{:T(128)}, bf16[2,512,12,64]{1,3,2,0:T(8,128)(2,1)S(1)}, bf16[2,512,12,64]{1,3,2,0:T(8,128)(2,1)}, ...), condition=%wide.region_10.11_spmd, body=%wide.region_7.10_spmd.sunk | while | flops 821428736 | bytes 28371012 | solution.py:83
  403.2 10.1 %fusion.105 = (f32[12,512]{1,0:T(8,128)S(1)}, f32[12,512,512]{1,2,0:T(8,128)}) fusion(bf16[2,512,12,64]{1,3,2,0:T(8,128)(2,1)} %get-tuple-element.108, s32[]{:T(128)} %get-tuple-element.98, bf16[2,512,12,64]{1,3,2,0:T(8,128)(2,1)} %get-tuple-element.107), kind=kOutput, calls=%fused_computation.82.clone.1 | convolution fusion | flops 412090880 | bytes 14181376 | tf_op jit(solution)/shard_map/while/body/eval_jaxpr/sub | solution.py:78
  413.3 6.0 %fusion.106 = bf16[2,512,12,64]{1,3,2,0:T(8,128)(2,1)S(1)} fusion(bf16[2,512,12,64]{1,3,2,0:T(8,128)(2,1)S(1)} %get-tuple-element.99, s32[]{:T(128)} %get-tuple-element.98, f32[12,512,512]{1,2,0:T(8,128)} %get-tuple-element.90, f32[12,512]{1,0:T(8,128)S(1)} %get-tuple-element.91, bf16[2,512,12,64]{1,3,2,0:T(8,128)(2,1)} %get-tuple-element.106), kind=kOutput, calls=%fused_computation.10.clone.1 | convolution fusion | flops 409337856 | bytes 14189568 | tf_op jit(solution)/shard_map/while/body/eval_jaxpr/hrs,shd->rhd/dot_general | solution.py:79
  419.4 10.1 %fusion.105 = (f32[12,512]{1,0:T(8,128)S(1)}, f32[12,512,512]{1,2,0:T(8,128)}) fusion(bf16[2,512,12,64]{1,3,2,0:T(8,128)(2,1)} %get-tuple-element.108, s32[]{:T(128)} %get-tuple-element.98, bf16[2,512,12,64]{1,3,2,0:T(8,128)(2,1)} %get-tuple-element.107), kind=kOutput, calls=%fused_computation.82.clone.1 | convolution fusion | flops 412090880 | bytes 14181376 | tf_op jit(solution)/shard_map/while/body/eval_jaxpr/sub | solution.py:78
  429.4 6.0 %fusion.106 = bf16[2,512,12,64]{1,3,2,0:T(8,128)(2,1)S(1)} fusion(bf16[2,512,12,64]{1,3,2,0:T(8,128)(2,1)S(1)} %get-tuple-element.99, s32[]{:T(128)} %get-tuple-element.98, f32[12,512,512]{1,2,0:T(8,128)} %get-tuple-element.90, f32[12,512]{1,0:T(8,128)S(1)} %get-tuple-element.91, bf16[2,512,12,64]{1,3,2,0:T(8,128)(2,1)} %get-tuple-element.106), kind=kOutput, calls=%fused_computation.10.clone.1 | convolution fusion | flops 409337856 | bytes 14189568 | tf_op jit(solution)/shard_map/while/body/eval_jaxpr/hrs,shd->rhd/dot_general | solution.py:79
  441.5 26.7 %all_to_all.119 = bf16[512,2,768]{2,1,0:T(2,128)(2,1)S(1)} all-to-all(bf16[512,2,768]{2,1,0:T(2,128)(2,1)S(1)} %copy.55), channel_id=1, replica_groups=mesh['seq'=16,'res'=8] {'seq'}, dimensions={0} | all-to-all | bytes 3145728 | tf_op jit(solution)/shard_map/all_to_all | solution.py:86
  471.6 5.4 %reshape.70 = f32[32,32,768]{2,1,0:T(8,128)} reshape(f32[32,16,2,768]{3,2,1,0:T(2,128)} %copy_bitcast_fusion) | data formatting | bytes 6291456 | tf_op jit(solution)/shard_map/convert_element_type | solution.py:87
  (53 shorter events, 56.1 us)
Async XLA Ops:
  6.5 287.9 %copy-start = (bf16[768,768]{1,0:T(8,128)(2,1)S(1)}, bf16[768,768]{1,0:T(8,128)(2,1)}, u32[]{:S(2)}) copy-start(bf16[768,768]{1,0:T(8,128)(2,1)} %param.15) | copy-start | bytes 3538948
  6.5 2.0 copy-start.2
  6.5 2.6 copy-start.6
  11.7 31.5 %all-to-all-start.1 = ((bf16[32,32,768]{2,1,0:T(8,128)(2,1)}), bf16[32,32,768]{2,1,0:T(8,128)(2,1)}, u32[]{:S(2)}, u32[]{:S(2)}) async-start(bf16[32,32,768]{2,1,0:T(8,128)(2,1)} %convolution_convert_fusion.5), calls=%async_computation.1 | async-start | bytes 3145728 | tf_op jit(solution)/shard_map/all_to_all | solution.py:38
  43.2 26.4 %all-to-all-start.2 = ((bf16[32,32,768]{2,1,0:T(8,128)(2,1)}), bf16[32,32,768]{2,1,0:T(8,128)(2,1)}, u32[]{:S(2)}, u32[]{:S(2)}) async-start(bf16[32,32,768]{2,1,0:T(8,128)(2,1)} %convolution_convert_fusion.4), calls=%async_computation.2 | async-start | bytes 3145728 | tf_op jit(solution)/shard_map/all_to_all | solution.py:39
  47.5 198.0 %all-reduce.2.cloned.1.call-start = ((), (), s32[]{:S(2)}) async-start(), calls=%async_computation.8 | async-start | bytes 6291456 | tf_op jit(solution)/shard_map/psum | solution.py:51
  295.9 3.4 copy-start.3
  296.0 1.8 copy-start.7
  301.3 27.8 %all-to-all-start.6 = ((bf16[32,32,768]{2,0,1:T(8,128)(2,1)}), bf16[32,32,768]{2,0,1:T(8,128)(2,1)S(1)}, u32[]{:S(2)}, u32[]{:S(2)}) async-start(bf16[32,32,768]{2,0,1:T(8,128)(2,1)} %copy.49), calls=%async_computation.6 | async-start | bytes 3145728 | tf_op jit(solution)/shard_map/all_to_all | solution.py:65
  329.1 26.5 %all-to-all-start.5 = ((bf16[32,32,768]{2,0,1:T(8,128)(2,1)}), bf16[32,32,768]{2,0,1:T(8,128)(2,1)}, u32[]{:S(2)}, u32[]{:S(2)}) async-start(bf16[32,32,768]{2,0,1:T(8,128)(2,1)} %copy.47), calls=%async_computation.5 | async-start | bytes 3145728 | tf_op jit(solution)/shard_map/all_to_all | solution.py:64
  355.7 36.7 %all-to-all-start.4 = ((bf16[32,32,768]{2,0,1:T(8,128)(2,1)}), bf16[32,32,768]{2,0,1:T(8,128)(2,1)}, u32[]{:S(2)}, u32[]{:S(2)}) async-start(bf16[32,32,768]{2,0,1:T(8,128)(2,1)} %copy.45), calls=%async_computation.4 | async-start | bytes 3145728 | tf_op jit(solution)/shard_map/all_to_all | solution.py:66
  397.8 5.5 %copy-start.5 = (bf16[2,512,12,64]{1,3,2,0:T(8,128)(2,1)S(1)}, bf16[2,512,12,64]{1,3,2,0:T(8,128)(2,1)}, u32[]{:S(2)}) copy-start(bf16[2,512,12,64]{1,3,2,0:T(8,128)(2,1)} %custom-call) | copy-start | bytes 4718596
  435.5 1.6 copy-start.8
  471.6 5.4 %copy-start.4 = (bf16[32,32,768]{2,1,0:T(8,128)(2,1)S(1)}, bf16[32,32,768]{2,1,0:T(8,128)(2,1)}, u32[]{:S(2)}) copy-start(bf16[32,32,768]{2,1,0:T(8,128)(2,1)} %copy-done.3) | copy-start | bytes 4718596
  477.0 3.6 copy-start.1
Sparse Core Ops, SparseCore 0:
  85.1 160.3 all-reduce.1
where the time goes:
time: 496 us; the launch traced here: 488 us
  waiting for transfers between devices  189 us (38%)
  local copies, waits for them, and re-layouts  81.2 us (16%)
  blocking collectives  79.4 us (16%)
  matrix products  72.8 us (15%)
  starting transfers between devices  37.3 us (8%)
  between operations  13.9 us (3%)
  other arithmetic  13.8 us (3%)
    psum x1, waiting for transfers between devices, on_device(): tied = lax.psum(partial_value, ('seq', 'res'))  124 us
    all_to_all x1, blocking collectives, on_device(): lax.all_to_all(v1, 'res', split_axis=0, concat_axis=1, tiled=True)  26.8 us
    all_to_all x1, blocking collectives, on_device(): lax.all_to_all(colupd, 'seq', split_axis=0, concat_axis=1, tiled=True)  26.7 us
    all_to_all x1, blocking collectives, on_device(): o1 = lax.all_to_all(o_moved, 'res', split_axis=1, concat_axis=0, tiled=True)  25.9 us
    dot_general x8, matrix products, project(): return jnp.dot(inputs, weight, preferred_element_type=jnp.float32)  21.4 us
    sub x2, matrix products, attend(): prob2 = jax.nn.softmax(score, axis=-1).astype(jnp.bfloat16)  20.1 us
    all_to_all x1, waiting for transfers between devices, on_device(): lax.all_to_all(q1, 'res', split_axis=0, concat_axis=1, tiled=True)  19.3 us
    reshape x3, local copies, waits for them, and re-layouts, split_heads(): return field.reshape(field.shape[0], field.shape[1], HEADS, D // HEADS)  17.7 us
  transfers between devices with their start and end apart: 6, of which 5 were waited for; matrix products, arithmetic and copies ran while one was open for 11% of the time, Pallas kernels for 0%

commit v1 on v0

--- a/solution.py
+++ b/solution.py
@@ -48,7 +48,8 @@
         )
         * tied_scale
     )
-    tied = lax.psum(partial_value, ("seq", "res"))
+    e_next = lax.psum(partial_value, "res")
+    tied = lax.psum(e_next, "seq")
     prob1 = jax.nn.softmax(tied, axis=-1).astype(jnp.bfloat16)
     o_moved = jnp.einsum(
         "hij,rjhd->rihd", prob1, split_heads(v_moved), preferred_element_type=jnp.float32

time: 496 us -> 614 us (1.24)
  waiting for transfers between devices: 189 us -> 305 us
    psum x1 -> x2, waiting for transfers between devices: 124 us -> 239 us  [the longest x1 144 us: on_device(): e_next = lax.psum(partial_value, 'res')]
  transfers between devices with their start and end apart: 6 -> 7, of which waited for: 5 -> 6; matrix products, arithmetic and copies ran while one was open for 11% -> 9% of each run, Pallas kernels for 0% -> 0%
where the time goes in v1:
time: 614 us; the launch traced here: 607 us
  waiting for transfers between devices  305 us (50%)
  blocking collectives  83.1 us (14%)
  local copies, waits for them, and re-layouts  81.2 us (13%)
  matrix products  72.8 us (12%)
  starting transfers between devices  37.2 us (6%)
  between operations  13.9 us (2%)
  other arithmetic  13.8 us (2%)
    psum x1, waiting for transfers between devices, on_device(): e_next = lax.psum(partial_value, 'res')  144 us
    psum x1, waiting for transfers between devices, on_device(): tied = lax.psum(e_next, 'seq')  94.9 us
    all_to_all x1, blocking collectives, on_device(): lax.all_to_all(v1, 'res', split_axis=0, concat_axis=1, tiled=True)  29.3 us
    all_to_all x1, blocking collectives, on_device(): o1 = lax.all_to_all(o_moved, 'res', split_axis=1, concat_axis=0, tiled=True)  27 us
    all_to_all x1, blocking collectives, on_device(): lax.all_to_all(colupd, 'seq', split_axis=0, concat_axis=1, tiled=True)  26.7 us
    dot_general x8, matrix products, project(): return jnp.dot(inputs, weight, preferred_element_type=jnp.float32)  21.4 us
    sub x2, matrix products, attend(): prob2 = jax.nn.softmax(score, axis=-1).astype(jnp.bfloat16)  20.1 us
    all_to_all x1, waiting for transfers between devices, on_device(): lax.all_to_all(q1, 'res', split_axis=0, concat_axis=1, tiled=True)  19.3 us
  transfers between devices with their start and end apart: 7, of which 6 were waited for; matrix products, arithmetic and copies ran while one was open for 9% of the time, Pallas kernels for 0%

profile of v1, /device:TPU:1, one launch (start us, length us, event | category | flops | bytes accessed | tf_op | source)
XLA Modules:
  0.0 606.6 jit_solution(15197584632654378315)
XLA Ops:
  11.7 8.3 %all-to-all-start.1 = ((bf16[32,32,768]{2,1,0:T(8,128)(2,1)}), bf16[32,32,768]{2,1,0:T(8,128)(2,1)}, u32[]{:S(2)}, u32[]{:S(2)}) async-start(bf16[32,32,768]{2,1,0:T(8,128)(2,1)} %convolution_convert_fusion.5), calls=%async_computation.1 | async-start | bytes 3145728 | tf_op jit(solution)/shard_map/all_to_all | solution.py:38
  20.1 3.9 convolution_convert_fusion.4
  23.9 19.3 %all-to-all-done.1 = bf16[32,32,768]{2,1,0:T(8,128)(2,1)} async-done(((bf16[32,32,768]{2,1,0:T(8,128)(2,1)}), bf16[32,32,768]{2,1,0:T(8,128)(2,1)}, u32[]{:S(2)}, u32[]{:S(2)}) %all-to-all-start.1) | async-done | bytes 1572896 | tf_op jit(solution)/shard_map/all_to_all | solution.py:38
  43.2 4.3 all-to-all-start.2
  50.3 5.9 reshape.63
  56.2 13.5 %all-to-all-done.2 = bf16[32,32,768]{2,1,0:T(8,128)(2,1)} async-done(((bf16[32,32,768]{2,1,0:T(8,128)(2,1)}), bf16[32,32,768]{2,1,0:T(8,128)(2,1)}, u32[]{:S(2)}, u32[]{:S(2)}) %all-to-all-start.2) | async-done | bytes 1572896 | tf_op jit(solution)/shard_map/all_to_all | solution.py:39
  72.3 5.9 reshape.64
  78.2 6.7 %bitcast_multiply_fusion = f32[12,256,256]{2,1,0:T(8,128)} fusion(bf16[4,256,12,64]{3,2,1,0:T(8,128)(2,1)} %reshape.64, bf16[4,256,12,64]{3,2,1,0:T(8,128)(2,1)} %reshape.63), kind=kOutput, calls=%fused_computation.43 | convolution fusion | flops 403439616 | bytes 6291456 | tf_op jit(solution)/shard_map/rihd,rjhd->hij/dot_general | solution.py:43
  85.0 144.2 %all-reduce.3.cloned.1.call-done = f32[12,256,256]{2,1,0:T(8,128)} async-done(((f32[12,256,256]{2,1,0:T(8,128)}), f32[12,256,256]{2,1,0:T(8,128)}) %all-reduce.3.cloned.1.call-update) | async-done | bytes 3145744 | tf_op jit(solution)/shard_map/psum | solution.py:51
  232.0 29.3 %all_to_all.117 = bf16[32,32,768]{2,1,0:T(8,128)(2,1)S(1)} all-to-all(bf16[32,32,768]{2,1,0:T(8,128)(2,1)S(1)} %convolution_convert_fusion.6), channel_id=1, replica_groups=mesh['seq'=16,'res'=8] {'res'}, dimensions={0} | all-to-all | bytes 3145728 | tf_op jit(solution)/shard_map/all_to_all | solution.py:40
  262.6 5.9 reshape.62
  268.4 94.9 %all-reduce.5.cloned.1.call-done = f32[12,256,256]{2,1,0:T(8,128)} async-done(((f32[12,256,256]{2,1,0:T(8,128)}), f32[12,256,256]{2,1,0:T(8,128)}) %all-reduce.5.cloned.1.call-update) | async-done | bytes 3145744 | tf_op jit(solution)/shard_map/psum | solution.py:52
  367.1 12.5 %fusion.63 = bf16[4,256,12,64]{1,3,0,2:T(8,128)(2,1)} fusion(f32[12,256]{1,0:T(8,128)S(1)} %fusion.92, bf16[4,256,12,64]{3,2,1,0:T(8,128)(2,1)} %reshape.62, f32[12,256,256]{2,1,0:T(8,128)} %all-reduce.5.cloned.1.call-done), kind=kOutput, calls=%fused_computation.68 | convolution fusion | flops 405802240 | bytes 6303744 | tf_op jit(solution)/shard_map/hij,rjhd->rihd/dot_general | solution.py:54
  386.0 27.0 %all_to_all.118 = bf16[4,256,768]{2,0,1:T(4,128)(2,1)S(1)} all-to-all(bf16[4,256,768]{2,0,1:T(4,128)(2,1)} %copy.42), channel_id=1, replica_groups=mesh['seq'=16,'res'=8] {'res'}, dimensions={1} | all-to-all | bytes 3145728 | tf_op jit(solution)/shard_map/all_to_all | solution.py:58
  420.3 6.2 %all-to-all-start.6 = ((bf16[32,32,768]{2,0,1:T(8,128)(2,1)}), bf16[32,32,768]{2,0,1:T(8,128)(2,1)S(1)}, u32[]{:S(2)}, u32[]{:S(2)}) async-start(bf16[32,32,768]{2,0,1:T(8,128)(2,1)} %copy.49), calls=%async_computation.6 | async-start | bytes 3145728 | tf_op jit(solution)/shard_map/all_to_all | solution.py:66
  431.7 16.4 %all-to-all-done.6 = bf16[32,32,768]{2,0,1:T(8,128)(2,1)S(1)} async-done(((bf16[32,32,768]{2,0,1:T(8,128)(2,1)}), bf16[32,32,768]{2,0,1:T(8,128)(2,1)S(1)}, u32[]{:S(2)}, u32[]{:S(2)}) %all-to-all-start.6) | async-done | bytes 1572896 | tf_op jit(solution)/shard_map/all_to_all | solution.py:66
  448.0 4.8 all-to-all-start.5
  458.1 16.4 %all-to-all-done.5 = bf16[32,32,768]{2,0,1:T(8,128)(2,1)} async-done(((bf16[32,32,768]{2,0,1:T(8,128)(2,1)}), bf16[32,32,768]{2,0,1:T(8,128)(2,1)}, u32[]{:S(2)}, u32[]{:S(2)}) %all-to-all-start.5) | async-done | bytes 1572896 | tf_op jit(solution)/shard_map/all_to_all | solution.py:65
  474.6 13.4 %all-to-all-start.4 = ((bf16[32,32,768]{2,0,1:T(8,128)(2,1)}), bf16[32,32,768]{2,0,1:T(8,128)(2,1)}, u32[]{:S(2)}, u32[]{:S(2)}) async-start(bf16[32,32,768]{2,0,1:T(8,128)(2,1)} %copy.45), calls=%async_computation.4 | async-start | bytes 3145728 | tf_op jit(solution)/shard_map/all_to_all | solution.py:67
  489.3 5.9 reshape.68
  495.2 5.3 copy.53
  502.0 3.9 reshape.67
  505.9 5.3 copy.52
  512.8 3.9 reshape.66
  516.6 5.5 copy.51
  522.1 32.3 %while.10 = (s32[]{:T(128)}, bf16[2,512,12,64]{1,3,2,0:T(8,128)(2,1)S(1)}, bf16[2,512,12,64]{1,3,2,0:T(8,128)(2,1)}, bf16[2,512,12,64]{1,3,2,0:T(8,128)(2,1)}, bf16[2,512,12,64]{1,3,2,0:T(8,128)(2,1)}, /*index=5*/s32[]{:T(128)}) while((s32[]{:T(128)}, bf16[2,512,12,64]{1,3,2,0:T(8,128)(2,1)S(1)}, bf16[2,512,12,64]{1,3,2,0:T(8,128)(2,1)}, ...), condition=%wide.region_11.12_spmd, body=%wide.region_8.11_spmd.sunk | while | flops 821428736 | bytes 28371012 | solution.py:84
  522.1 10.1 %fusion.105 = (f32[12,512]{1,0:T(8,128)S(1)}, f32[12,512,512]{1,2,0:T(8,128)}) fusion(bf16[2,512,12,64]{1,3,2,0:T(8,128)(2,1)} %get-tuple-element.108, s32[]{:T(128)} %get-tuple-element.98, bf16[2,512,12,64]{1,3,2,0:T(8,128)(2,1)} %get-tuple-element.107), kind=kOutput, calls=%fused_computation.82.clone.1 | convolution fusion | flops 412090880 | bytes 14181376 | tf_op jit(solution)/shard_map/while/body/eval_jaxpr/sub | solution.py:79
  532.2 6.0 fusion.106
  538.2 10.1 %fusion.105 = (f32[12,512]{1,0:T(8,128)S(1)}, f32[12,512,512]{1,2,0:T(8,128)}) fusion(bf16[2,512,12,64]{1,3,2,0:T(8,128)(2,1)} %get-tuple-element.108, s32[]{:T(128)} %get-tuple-element.98, bf16[2,512,12,64]{1,3,2,0:T(8,128)(2,1)} %get-tuple-element.107), kind=kOutput, calls=%fused_computation.82.clone.1 | convolution fusion | flops 412090880 | bytes 14181376 | tf_op jit(solution)/shard_map/while/body/eval_jaxpr/sub | solution.py:79
  548.3 6.0 fusion.106
  560.4 26.7 %all_to_all.119 = bf16[512,2,768]{2,1,0:T(2,128)(2,1)S(1)} all-to-all(bf16[512,2,768]{2,1,0:T(2,128)(2,1)S(1)} %copy.55), channel_id=1, replica_groups=mesh['seq'=16,'res'=8] {'seq'}, dimensions={0} | all-to-all | bytes 3145728 | tf_op jit(solution)/shard_map/all_to_all | solution.py:87
  590.5 5.4 reshape.70
  (56 shorter events, 59.9 us)
Async XLA Ops:
  6.5 406.9 %copy-start = (bf16[768,768]{1,0:T(8,128)(2,1)S(1)}, bf16[768,768]{1,0:T(8,128)(2,1)}, u32[]{:S(2)}) copy-start(bf16[768,768]{1,0:T(8,128)(2,1)} %param.15) | copy-start | bytes 3538948
  6.5 2.0 copy-start.2
  6.5 2.6 copy-start.6
  11.7 31.5 %all-to-all-start.1 = ((bf16[32,32,768]{2,1,0:T(8,128)(2,1)}), bf16[32,32,768]{2,1,0:T(8,128)(2,1)}, u32[]{:S(2)}, u32[]{:S(2)}) async-start(bf16[32,32,768]{2,1,0:T(8,128)(2,1)} %convolution_convert_fusion.5), calls=%async_computation.1 | async-start | bytes 3145728 | tf_op jit(solution)/shard_map/all_to_all | solution.py:38
  43.2 26.4 %all-to-all-start.2 = ((bf16[32,32,768]{2,1,0:T(8,128)(2,1)}), bf16[32,32,768]{2,1,0:T(8,128)(2,1)}, u32[]{:S(2)}, u32[]{:S(2)}) async-start(bf16[32,32,768]{2,1,0:T(8,128)(2,1)} %convolution_convert_fusion.4), calls=%async_computation.2 | async-start | bytes 3145728 | tf_op jit(solution)/shard_map/all_to_all | solution.py:39
  47.5 181.7 %all-reduce.3.cloned.1.call-start = ((), (), s32[]{:S(2)}) async-start(), calls=%async_computation.8 | async-start | bytes 6291456 | tf_op jit(solution)/shard_map/psum | solution.py:51
  85.0 278.3 %all-reduce.5.cloned.1.call-start = ((), (), s32[]{:S(2)}) async-start(), calls=%async_computation.9 | async-start | bytes 6291456 | tf_op jit(solution)/shard_map/psum | solution.py:52
  414.9 3.3 copy-start.3
  414.9 1.8 copy-start.7
  420.3 27.7 %all-to-all-start.6 = ((bf16[32,32,768]{2,0,1:T(8,128)(2,1)}), bf16[32,32,768]{2,0,1:T(8,128)(2,1)S(1)}, u32[]{:S(2)}, u32[]{:S(2)}) async-start(bf16[32,32,768]{2,0,1:T(8,128)(2,1)} %copy.49), calls=%async_computation.6 | async-start | bytes 3145728 | tf_op jit(solution)/shard_map/all_to_all | solution.py:66
  448.0 26.5 %all-to-all-start.5 = ((bf16[32,32,768]{2,0,1:T(8,128)(2,1)}), bf16[32,32,768]{2,0,1:T(8,128)(2,1)}, u32[]{:S(2)}, u32[]{:S(2)}) async-start(bf16[32,32,768]{2,0,1:T(8,128)(2,1)} %copy.47), calls=%async_computation.5 | async-start | bytes 3145728 | tf_op jit(solution)/shard_map/all_to_all | solution.py:65
  474.6 36.7 %all-to-all-start.4 = ((bf16[32,32,768]{2,0,1:T(8,128)(2,1)}), bf16[32,32,768]{2,0,1:T(8,128)(2,1)}, u32[]{:S(2)}, u32[]{:S(2)}) async-start(bf16[32,32,768]{2,0,1:T(8,128)(2,1)} %copy.45), calls=%async_computation.4 | async-start | bytes 3145728 | tf_op jit(solution)/shard_map/all_to_all | solution.py:67
  516.6 5.5 copy-start.5
  554.4 1.6 copy-start.8
  590.5 5.4 copy-start.4
  595.9 3.6 copy-start.1
Sparse Core Ops, SparseCore 0:
  85.1 144.0 all-reduce.2
  231.7 131.5 all-reduce.4
